TPU v7x, 32 devices: a whole 2x2x4 slice. The times are simulated.
32 devices in a mesh: dp: 16 (over z, y, core), ctx: 2 (over x).
Axes of the slice: x: 2, y: 2, z: 4, core: 2. Of those that a mesh axis runs over, the one named last changes fastest.
Arguments:
- conv_input: bfloat16 [16, 256, 4096], P('dp', 'ctx'), may hold values from -6 to 6
- gate_value: bfloat16 [16, 256, 4096], P('dp', 'ctx'), may hold values from -6 to 6
- out_grad: bfloat16 [16, 256, 4096], P('dp', 'ctx'), may hold values from -6 to 6
- filter_taps: bfloat16 [128, 4096], P('dp'), may hold values from -0.5 to 0.5
Outputs:
- input_grad: bfloat16 [16, 256, 4096], P('dp', 'ctx')
- filter_grad: float32 [128, 4096], P('dp')
All inputs are finite; a program needn't handle non-finite values.
Results may differ from a plain program's by a relative error of at most 0.0051.
Values may be sent and summed in bfloat16 or wider, within the bound.
A program may use at most 64 MiB of HBM per device.

v0:
```python
import math
import jax
import jax.numpy as jnp
from jax import lax
from jax.sharding import PartitionSpec as P

TAPS = 128


def from_behind(block, axis, distance):
    devices = range(lax.axis_size(axis))
    route = [(i - distance, i) for i in devices if i - distance in devices]
    return lax.ppermute(block, axis, route)


def correlate(signal, kernel):
    return lax.conv_general_dilated(
        signal[None],
        kernel[:, None, :],
        (1,),
        "VALID",
        dimension_numbers=("NWC", "WIO", "NWC"),
        feature_group_count=signal.shape[1],
        preferred_element_type=jnp.float32,
    )[0]


def shards(conv_input, gate_value, out_grad, filter_taps):
    inputs = conv_input[0]
    rows = inputs.shape[0]
    mixed = (out_grad[0].astype(jnp.float32) * gate_value[0].astype(jnp.float32)).astype(
        jnp.bfloat16
    )
    rim_rows = from_behind(mixed[: TAPS - 1], "ctx", -1)
    grad_ext = jnp.concatenate([mixed, rim_rows], 0)
    partial_grad = correlate(grad_ext, inputs)
    full_taps = lax.all_gather(filter_taps, "dp", axis=0, tiled=True)
    back_sum = correlate(grad_ext, full_taps)
    summed = lax.psum(partial_grad, "ctx")
    shard_grad = lax.psum_scatter(summed, "dp", scatter_dimension=0, tiled=True)
    tokens_all = rows * lax.axis_size("ctx") * lax.axis_size("dp")
    scale_factor = 1.0 / math.sqrt(tokens_all)
    return (back_sum.astype(jnp.bfloat16)[None], shard_grad * scale_factor)


def solution(mesh):
    in_specs = (P("dp", "ctx", None), P("dp", "ctx", None), P("dp", "ctx", None), P("dp", None))
    out_specs = (P("dp", "ctx", None), P("dp", None))
    return jax.shard_map(shards, mesh=mesh, in_specs=in_specs, out_specs=out_specs, check_vma=False)
```

profile of v0, /device:TPU:0, one launch (start us, length us, event | category | flops | bytes accessed | tf_op | source)
XLA Modules:
  0.0 211.5 jit_solution(7849527368872966788)
XLA Ops:
  7.2 0.0 copy-start
  7.2 0.0 reduce-scatter.2.cloned.1.call-start
  7.2 1.9 multiply_convert_fusion
  9.2 0.1 slice_bitcast_fusion
  9.2 1.3 collective-permute-start
  10.5 26.2 %collective-permute-done = bf16[127,4096]{1,0:T(8,128)(2,1)S(1)} collective-permute-done((bf16[127,4096]{1,0:T(8,128)(2,1)S(1)}, bf16[127,4096]{1,0:T(8,128)(2,1)S(1)}, u32[]{:S(2)}, u32[]{:S(2)}) %collective-permute-start) | collective-permute-done | bytes 1040416 | tf_op jit(solution)/shard_map/ppermute | solution.py:13
  36.7 0.2 maximum_bitcast_fusion
  36.9 0.0 copy-done
  36.9 30.1 %fusion = f32[1,128,4096]{2,0,1:T(1,128)S(1)} fusion(bf16[1,255,4096]{2,1,0:T(8,128)(2,1)S(1)} %maximum_bitcast_fusion, bf16[128,1,4096]{2,0,1:T(8,128)(2,1)S(1)} %bitcast.10), kind=kOutput, calls=%fused_computation.1 | convolution fusion | flops 134217728 | bytes 5234688 | tf_op jit(solution)/shard_map/conv_general_dilated | solution.py:17
  67.0 3.0 %copy.23 = f32[1,128,4096]{2,1,0:T(8,128)} copy(f32[1,128,4096]{2,0,1:T(1,128)S(1)} %fusion) | data formatting | bytes 4194304
  70.0 0.0 reduce-scatter.2.cloned.1.call-update
  70.0 0.0 all-gather.2.cloned.1.call-start
  70.1 0.7 all-gather.2.cloned.1.call-update
  70.8 0.0 all-reduce.2.cloned.1.call-start
  70.8 62.3 %reduce-scatter.2.cloned.1.call-done = f32[8,4096]{1,0:T(8,128)} async-done(((f32[128,4096]{1,0:T(8,128)}), f32[8,4096]{1,0:T(8,128)}) %reduce-scatter.2.cloned.1.call-update) | async-done | bytes 131088 | tf_op jit(solution)/shard_map/reduce_scatter | solution.py:40
  133.1 0.0 all-reduce.2.cloned.1.call-update
  133.2 39.0 %all-gather.2.cloned.1.call-done = bf16[128,4096]{1,0:T(8,128)(2,1)} async-done(((bf16[8,4096]{1,0:T(8,128)(2,1)}), bf16[128,4096]{1,0:T(8,128)(2,1)}) %all-gather.2.cloned.1.call-update) | async-done | bytes 1048592 | tf_op jit(solution)/shard_map/all_gather | solution.py:37
  172.2 29.1 %convolution_convert_fusion = bf16[1,128,4096]{2,0,1:T(2,128)(2,1)S(1)} fusion(bf16[1,255,4096]{2,1,0:T(8,128)(2,1)S(1)} %maximum_bitcast_fusion, bf16[128,1,4096]{2,0,1:T(8,128)(2,1)} %bitcast.13), kind=kOutput, calls=%fused_computation | convolution fusion | flops 134742016 | bytes 4186112 | tf_op jit(solution)/shard_map/conv_general_dilated | solution.py:17
  201.3 2.1 copy.12
  203.4 0.0 all-reduce.2.cloned.1.call-done
  203.4 1.6 broadcast_multiply_fusion
Async XLA Ops:
  7.2 29.8 %copy-start = (bf16[1,128,4096]{2,1,0:T(8,128)(2,1)S(1)}, bf16[1,128,4096]{2,1,0:T(8,128)(2,1)}, u32[]{:S(2)}) copy-start(bf16[1,128,4096]{2,1,0:T(8,128)(2,1)} %param.4) | copy-start | bytes 3145732
  7.2 126.0 %reduce-scatter.2.cloned.1.call-start = ((), (), s32[]{:S(2)}) async-start(), calls=%async_computation.2 | async-start | bytes 2228224 | tf_op jit(solution)/shard_map/reduce_scatter | solution.py:40
  9.2 27.5 %collective-permute-start = (bf16[127,4096]{1,0:T(8,128)(2,1)S(1)}, bf16[127,4096]{1,0:T(8,128)(2,1)S(1)}, u32[]{:S(2)}, u32[]{:S(2)}) collective-permute-start(bf16[127,4096]{1,0:T(8,128)(2,1)S(1)} %slice_bitcast_fusion), channel_id=1, source_target_pairs={{1,0},{3,2},{5,4},{7,6},{9,8},{11,10},{13,12},{15,14},{17,16},{19,... | collective-permute-start | bytes 3121160 | tf_op jit(solution)/shard_map/ppermute | solution.py:13
  70.0 102.1 %all-gather.2.cloned.1.call-start = ((), (), s32[]{:S(2)}) async-start(), calls=%async_computation.1 | async-start | bytes 1114112 | tf_op jit(solution)/shard_map/all_gather | solution.py:37
  70.8 132.6 %all-reduce.2.cloned.1.call-start = ((), (), s32[]{:S(2)}) async-start(), calls=%async_computation.3 | async-start | bytes 262144 | tf_op jit(solution)/shard_map/psum | solution.py:39
Sparse Core Ops, SparseCore 0:
  70.2 62.9 reduce-scatter.1
  135.3 36.8 all-gather.1
  174.4 20.4 all-reduce.1
where the time goes:
time: 212 us; the launch traced here: 211 us
  waiting for transfers between devices  128 us (60%)
  matrix products  59.2 us (28%)
  between operations  13.8 us (7%)
  local copies, waits for them, and re-layouts  5.18 us (2%)
  other arithmetic  3.71 us (2%)
    reduce_scatter x1, waiting for transfers between devices, shards(): shard_grad = lax.psum_scatter(summed, 'dp', scatter_dimension=0, tiled=True)  62.3 us
    conv_general_dilated x2, matrix products, correlate(): lax.conv_general_dilated(signal[None], kernel[:, None, :], (1,), 'VALID',...  59.2 us
    all_gather x1, waiting for transfers between devices, shards(): full_taps = lax.all_gather(filter_taps, 'dp', axis=0, tiled=True)  39 us
    ppermute x1, waiting for transfers between devices, from_behind(): return lax.ppermute(block, axis, route)  26.2 us
    unnamed x4, local copies, waits for them, and re-layouts  5.1 us
  transfers between devices with their start and end apart: 4, of which 3 were waited for; matrix products, arithmetic and copies ran while one was open for 15% of the time, Pallas kernels for 0%

commit v1 on v0

--- a/solution.py
+++ b/solution.py
@@ -34,7 +34,9 @@
     rim_rows = from_behind(mixed[: TAPS - 1], "ctx", -1)
     grad_ext = jnp.concatenate([mixed, rim_rows], 0)
     partial_grad = correlate(grad_ext, inputs)
-    full_taps = lax.all_gather(filter_taps, "dp", axis=0, tiled=True)
+    full_taps = jnp.concatenate(
+        lax.all_to_all(jnp.stack([filter_taps] * lax.axis_size("dp")), "dp", 0, 0), axis=0
+    )
     back_sum = correlate(grad_ext, full_taps)
     summed = lax.psum(partial_grad, "ctx")
     shard_grad = lax.psum_scatter(summed, "dp", scatter_dimension=0, tiled=True)

time: 212 us -> 174 us (0.82)
  waiting for transfers between devices: 128 us -> 81.8 us
  starting transfers between devices: 1.41 us -> 8.18 us
    all_gather x1 -> x0, waiting for transfers between devices: 39 us -> none  [shards(): full_taps = lax.all_gather(filter_taps, 'dp', axis=0, tiled=True)]
    all_to_all x0 -> x1, starting transfers between devices: none -> 6.81 us  [shards(): lax.all_to_all(jnp.stack([filter_taps] * lax.axis_size('dp')), 'dp', 0, 0)]
    reduce_scatter x1, waiting for transfers between devices: 62.3 us -> 55.6 us  [shards(): shard_grad = lax.psum_scatter(summed, 'dp', scatter_dimension=0, tiled=True)]
    unnamed x4 -> x6, local copies, waits for them, and re-layouts: 5.1 us -> 5.91 us
  transfers between devices with their start and end apart: 4 -> 4, of which waited for: 3 -> 2; matrix products, arithmetic and copies ran while one was open for 15% -> 19% of each run, Pallas kernels for 0% -> 0%
where the time goes in v1:
time: 174 us
  waiting for transfers between devices  81.8 us (47%)
  matrix products  59.2 us (34%)
  between operations  14.1 us (8%)
  starting transfers between devices  8.18 us (5%)
  local copies, waits for them, and re-layouts  7.06 us (4%)
  other arithmetic  3.71 us (2%)
    conv_general_dilated x2, matrix products, correlate(): lax.conv_general_dilated(signal[None], kernel[:, None, :], (1,), 'VALID',...  59.2 us
    reduce_scatter x1, waiting for transfers between devices, shards(): shard_grad = lax.psum_scatter(summed, 'dp', scatter_dimension=0, tiled=True)  55.6 us
    ppermute x1, waiting for transfers between devices, from_behind(): return lax.ppermute(block, axis, route)  26.2 us
    all_to_all x1, starting transfers between devices, shards(): lax.all_to_all(jnp.stack([filter_taps] * lax.axis_size('dp')), 'dp', 0, 0)  6.81 us
    unnamed x6, local copies, waits for them, and re-layouts  5.91 us
  transfers between devices with their start and end apart: 4, of which 2 were waited for; matrix products, arithmetic and copies ran while one was open for 19% of the time, Pallas kernels for 0%

profile of v1, /device:TPU:0, one launch (start us, length us, event | category | flops | bytes accessed | tf_op | source)
XLA Modules:
  0.0 174.0 jit_solution(12907940087298782318)
XLA Ops:
  7.2 0.0 copy-start
  7.2 0.0 reduce-scatter.2.cloned.1.call-start
  7.2 1.9 %multiply_convert_fusion = bf16[1,128,4096]{2,1,0:T(8,128)(2,1)S(1)} fusion(bf16[1,128,4096]{2,1,0:T(8,128)(2,1)} %param.5, bf16[1,128,4096]{2,1,0:T(8,128)(2,1)} %param.6), kind=kLoop, calls=%fused_computation.8 | loop fusion | flops 2097152 | bytes 3145728 | tf_op jit(solution)/shard_map/convert_element_type | solution.py:31
  9.2 0.1 slice_bitcast_fusion
  9.2 1.3 collective-permute-start
  10.5 26.2 %collective-permute-done = bf16[127,4096]{1,0:T(8,128)(2,1)S(1)} collective-permute-done((bf16[127,4096]{1,0:T(8,128)(2,1)S(1)}, bf16[127,4096]{1,0:T(8,128)(2,1)S(1)}, u32[]{:S(2)}, u32[]{:S(2)}) %collective-permute-start) | collective-permute-done | bytes 1040416 | tf_op jit(solution)/shard_map/ppermute | solution.py:13
  36.7 0.2 maximum_bitcast_fusion
  36.9 0.0 copy-done
  36.9 30.1 %fusion = f32[1,128,4096]{2,0,1:T(1,128)S(1)} fusion(bf16[1,255,4096]{2,1,0:T(8,128)(2,1)S(1)} %maximum_bitcast_fusion, bf16[128,1,4096]{2,0,1:T(8,128)(2,1)S(1)} %bitcast.10), kind=kOutput, calls=%fused_computation.1 | convolution fusion | flops 134217728 | bytes 5234688 | tf_op jit(solution)/shard_map/conv_general_dilated | solution.py:17
  67.0 3.0 %copy.23 = f32[1,128,4096]{2,1,0:T(8,128)} copy(f32[1,128,4096]{2,0,1:T(1,128)S(1)} %fusion) | data formatting | bytes 4194304
  70.0 0.0 copy-start.1
  70.0 0.0 reduce-scatter.2.cloned.1.call-update
  70.1 0.8 copy-done.1
  70.9 1.1 stack.2
  71.9 6.8 %all-to-all-start = ((bf16[16,8,4096]{2,1,0:T(8,128)(2,1)}), bf16[16,8,4096]{2,1,0:T(8,128)(2,1)}, u32[]{:S(2)}, u32[]{:S(2)}) async-start(bf16[16,8,4096]{2,1,0:T(8,128)(2,1)} %stack.2), calls=%async_computation | async-start | bytes 2097152 | tf_op jit(solution)/shard_map/all_to_all | solution.py:38
  78.8 0.0 all-reduce.2.cloned.1.call-start
  78.8 55.6 %reduce-scatter.2.cloned.1.call-done = f32[8,4096]{1,0:T(8,128)} async-done(((f32[128,4096]{1,0:T(8,128)}), f32[8,4096]{1,0:T(8,128)}) %reduce-scatter.2.cloned.1.call-update) | async-done | bytes 131088 | tf_op jit(solution)/shard_map/reduce_scatter | solution.py:42
  134.4 0.0 all-reduce.2.cloned.1.call-update
  134.4 0.0 all-to-all-done
  134.4 29.1 %convolution_convert_fusion = bf16[1,128,4096]{2,0,1:T(2,128)(2,1)S(1)} fusion(bf16[1,255,4096]{2,1,0:T(8,128)(2,1)S(1)} %maximum_bitcast_fusion, bf16[128,1,4096]{2,0,1:T(8,128)(2,1)} %bitcast.3), kind=kOutput, calls=%fused_computation | convolution fusion | flops 134742016 | bytes 4186112 | tf_op jit(solution)/shard_map/conv_general_dilated | solution.py:17
  163.5 2.1 %copy.12 = bf16[1,128,4096]{2,1,0:T(8,128)(2,1)} copy(bf16[1,128,4096]{2,0,1:T(2,128)(2,1)S(1)} %convolution_convert_fusion) | data formatting | bytes 2097152
  165.6 0.0 all-reduce.2.cloned.1.call-done
  165.6 1.6 broadcast_multiply_fusion
Async XLA Ops:
  7.2 29.8 %copy-start = (bf16[1,128,4096]{2,1,0:T(8,128)(2,1)S(1)}, bf16[1,128,4096]{2,1,0:T(8,128)(2,1)}, u32[]{:S(2)}) copy-start(bf16[1,128,4096]{2,1,0:T(8,128)(2,1)} %param.4) | copy-start | bytes 3145732
  7.2 127.2 %reduce-scatter.2.cloned.1.call-start = ((), (), s32[]{:S(2)}) async-start(), calls=%async_computation.2 | async-start | bytes 2228224 | tf_op jit(solution)/shard_map/reduce_scatter | solution.py:42
  9.2 27.5 %collective-permute-start = (bf16[127,4096]{1,0:T(8,128)(2,1)S(1)}, bf16[127,4096]{1,0:T(8,128)(2,1)S(1)}, u32[]{:S(2)}, u32[]{:S(2)}) collective-permute-start(bf16[127,4096]{1,0:T(8,128)(2,1)S(1)} %slice_bitcast_fusion), channel_id=1, source_target_pairs={{1,0},{3,2},{5,4},{7,6},{9,8},{11,10},{13,12},{15,14},{17,16},{19,... | collective-permute-start | bytes 3121160 | tf_op jit(solution)/shard_map/ppermute | solution.py:13
  70.0 0.8 copy-start.1
  71.9 62.5 %all-to-all-start = ((bf16[16,8,4096]{2,1,0:T(8,128)(2,1)}), bf16[16,8,4096]{2,1,0:T(8,128)(2,1)}, u32[]{:S(2)}, u32[]{:S(2)}) async-start(bf16[16,8,4096]{2,1,0:T(8,128)(2,1)} %stack.2), calls=%async_computation | async-start | bytes 2097152 | tf_op jit(solution)/shard_map/all_to_all | solution.py:38
  78.8 86.9 %all-reduce.2.cloned.1.call-start = ((), (), s32[]{:S(2)}) async-start(), calls=%async_computation.3 | async-start | bytes 262144 | tf_op jit(solution)/shard_map/psum | solution.py:41
Sparse Core Ops, SparseCore 0:
  70.2 64.1 reduce-scatter.1
  136.6 20.4 all-reduce.1
